TPU v7x, 512 devices: a whole 4x8x8 slice. The times are simulated.
512 devices in a mesh: gx: 16 (over x, z_hi), gy: 32 (over y, z_lo, core).
Axes of the slice: x: 4, y: 8, z: 8 (z_hi: 4, z_lo: 2; z = z_hi * 2 + z_lo), core: 2. Of those that a mesh axis runs over, the one named last changes fastest.
Arguments:
- prev_block: float32 [3, 8, 128, 256, 128], P(None, None, 'gx', 'gy'), may hold values from -20 to 20
- block: float32 [3, 8, 128, 256, 128], P(None, None, 'gx', 'gy'), may hold values from -20 to 20
- hop_seed: int32 [3, 128, 256, 128], P(None, 'gx', 'gy'), may hold values from 0 to 15
- levels: int32 [128, 256, 128], P('gx', 'gy'), may hold values from 0 to 15
- hop_table: float32 [3, 16, 3, 3], replicated, may hold values from -3 to 3
- onsite_table: float32 [16, 3], replicated, may hold values from -2 to 2
Outputs:
- next_block: float32 [3, 8, 128, 256, 128], P(None, None, 'gx', 'gy')
- alpha: float32 [8, 8], replicated
- beta: float32 [8, 8], replicated
All inputs are finite; a program needn't handle non-finite values.
Results may differ from a plain program's by a relative error of at most 0.0003.
Values sent between devices are 32-bit elements; how exact they have to be, the bound alone decides.
A program may use at most 64 MiB of HBM per device.

v0:
```python
import jax
import jax.numpy as jnp
from jax import lax
from jax.sharding import PartitionSpec as P

HIGH = lax.Precision.HIGHEST


def extended(value, sides, width):
    for axis, dim in sides:
        count, length = (lax.axis_size(axis), value.shape[dim])
        up = [(i, (i + 1) % count) for i in range(count)]
        down = [(j, i) for i, j in up]
        last = lax.slice_in_dim(value, length - width, length, axis=dim)
        leading = lax.slice_in_dim(value, 0, width, axis=dim)
        before = lax.ppermute(last, axis, up)
        after = lax.ppermute(leading, axis, down)
        value = jnp.concatenate([before, value, after], axis=dim)
    return value


def passed_along(value, axis, steps):
    count = lax.axis_size(axis)
    pairs = [(source, (source + steps) % count) for source in range(count)]
    return lax.ppermute(value, axis, pairs)


def table_rows(table_flat, indices):
    entries = table_flat.shape[0]
    flat = indices.reshape(-1)
    onehot = (flat[None, :] == jnp.arange(entries, dtype=jnp.int32)[:, None]).astype(jnp.float32)
    picked = lax.dot_general(table_flat, onehot, (((0,), (0,)), ((), ())), precision=HIGH)
    return picked.reshape((table_flat.shape[1],) + indices.shape)


def hop_blocks(table_dir, seeds):
    orbs = table_dir.shape[1]
    picked = table_rows(table_dir.reshape(table_dir.shape[0], orbs * orbs), seeds)
    return picked.reshape((orbs, orbs) + seeds.shape)


def forward(bonds, field):
    orbs = field.shape[0]
    rows = []
    for left in range(orbs):
        acc = bonds[left, 0][None] * field[0]
        for right in range(1, orbs):
            acc = acc + bonds[left, right][None] * field[right]
        rows.append(acc)
    return jnp.stack(rows, axis=0)


def backward(bonds, field):
    orbs = field.shape[0]
    rows = []
    for right in range(orbs):
        acc = bonds[0, right][None] * field[0]
        for left in range(1, orbs):
            acc = acc + bonds[left, right][None] * field[left]
        rows.append(acc)
    return jnp.stack(rows, axis=0)


def onsite_image(block, levels, onsite_table):
    energy = table_rows(onsite_table, levels)
    return energy[:, None] * block


def apply_values(block, hop_seed, levels, hop_table, onsite_table):
    padded = extended(block, (("gx", 2), ("gy", 3)), 1)
    ahead = [padded[:, :, 2:, 1:-1], padded[:, :, 1:-1, 2:], jnp.roll(block, -1, axis=4)]
    behind = [padded[:, :, :-2, 1:-1], padded[:, :, 1:-1, :-2], jnp.roll(block, 1, axis=4)]
    edge_x = passed_along(hop_seed[0, -1:], "gx", 1)
    edge_y = passed_along(hop_seed[1, :, -1:], "gy", 1)
    seeds_behind = [
        jnp.concatenate([edge_x, hop_seed[0, :-1]], axis=0),
        jnp.concatenate([edge_y, hop_seed[1, :, :-1]], axis=1),
        jnp.roll(hop_seed[2], 1, axis=2),
    ]
    image = onsite_image(block, levels, onsite_table)
    for direction in range(3):
        image = image + forward(
            hop_blocks(hop_table[direction], hop_seed[direction]), ahead[direction]
        )
        image = image + backward(
            hop_blocks(hop_table[direction], seeds_behind[direction]), behind[direction]
        )
    return image


def local_inner(left, right):
    total = None
    for orbit in range(left.shape[0]):
        flat_left = left[orbit].reshape(left.shape[1], -1)
        flat_right = right[orbit].reshape(right.shape[1], -1)
        part_sum = lax.dot_general(flat_left, flat_right, (((1,), (1,)), ((), ())), precision=HIGH)
        total = part_sum if total is None else total + part_sum
    return total


def apply_left(matrix, field):
    rows = []
    for orbit in range(field.shape[0]):
        flat = field[orbit].reshape(field.shape[1], -1)
        mixed = jnp.dot(matrix, flat, precision=HIGH)
        rows.append(mixed.reshape((matrix.shape[0],) + field.shape[2:]))
    return jnp.stack(rows, axis=0)


def combine(basis, coeffs):
    return apply_left(coeffs.T, basis)


def per_device(prev_block, block, hop_seed, levels, hop_table, onsite_table):
    count = (
        block.shape[0]
        * block.shape[2]
        * block.shape[3]
        * block.shape[4]
        * lax.axis_size("gx")
        * lax.axis_size("gy")
    )
    product = apply_values(block, hop_seed, levels, hop_table, onsite_table)
    basis = jnp.concatenate([prev_block, block], axis=1)
    width = block.shape[1]
    first = lax.psum(local_inner(basis, product), ("gx", "gy")) / count
    residual_one = product - combine(basis, first)
    second = lax.psum(local_inner(basis, residual_one), ("gx", "gy")) / count
    residual_two = residual_one - combine(basis, second)
    gram = lax.psum(local_inner(residual_two, residual_two), ("gx", "gy")) / count
    alpha = first[width:]
    lower = jnp.linalg.cholesky(gram)
    lower_inv = jax.scipy.linalg.solve_triangular(
        lower, jnp.eye(width, dtype=jnp.float32), lower=True
    )
    next_block = apply_left(lower_inv, residual_two)
    return (next_block, alpha, lower.T)


def solution(mesh):
    in_specs = (
        P(None, None, "gx", "gy", None),
        P(None, None, "gx", "gy", None),
        P(None, "gx", "gy", None),
        P("gx", "gy", None),
        P(),
        P(),
    )
    out_specs = (P(None, None, "gx", "gy", None), P(), P())
    return jax.shard_map(
        per_device, mesh=mesh, in_specs=in_specs, out_specs=out_specs, check_vma=False
    )
```

profile of v0, /device:TPU:1, one launch (start us, length us, event | category | flops | bytes accessed | tf_op | source)
XLA Modules:
  0.0 391.7 jit_solution(6826044836774343264)
XLA Ops:
  2.3 6.6 %collective-permute-start.2 = (f32[3,8,1,8,128]{4,1,3,2,0:T(8,128)}, f32[3,8,1,8,128]{4,1,3,2,0:T(8,128)}, u32[]{:S(2)}, u32[]{:S(2)}) collective-permute-start(f32[3,8,1,8,128]{4,1,3,2,0:T(8,128)} %copy.105), channel_id=1, source_target_pairs={{0,32},{32,64},{64,96},{96,128},{128,160},{160,192},{192,224},{224... | collective-permute-start | bytes 294920 | tf_op jit(solution)/shard_map/ppermute | solution.py:16
  9.6 9.0 %collective-permute-start = (f32[3,8,1,8,128]{4,1,3,2,0:T(8,128)}, f32[3,8,1,8,128]{4,1,3,2,0:T(8,128)}, u32[]{:S(2)}, u32[]{:S(2)}) collective-permute-start(f32[3,8,1,8,128]{4,1,3,2,0:T(8,128)} %copy.104), channel_id=1, source_target_pairs={{32,0},{64,32},{96,64},{128,96},{160,128},{192,160},{224,192},{256... | collective-permute-start | bytes 294920 | tf_op jit(solution)/shard_map/ppermute | solution.py:17
  18.6 1.4 slice.453
  20.0 3.9 %collective-permute-start.4 = (s32[8,1,128]{2,0,1:T(8,128)}, s32[8,1,128]{2,0,1:T(8,128)}, u32[]{:S(2)}, u32[]{:S(2)}) collective-permute-start(s32[8,1,128]{2,0,1:T(8,128)} %bitcast.37), channel_id=1, source_target_pairs={{0,1},{1,2},{2,3},{3,4},{4,5},{5,6},{6,7},{7,8},{8,9},{9,10},{10,1... | collective-permute-start | bytes 12296 | tf_op jit(solution)/shard_map/ppermute | solution.py:25
  23.9 1.3 slice_bitcast_fusion.72
  25.2 1.9 collective-permute-start.1
  32.9 1.6 copy.108
  34.5 1.3 copy.109
  37.0 1.4 copy.106
  38.4 1.3 copy.107
  42.6 1.8 multiply_add_fusion.2
  44.5 1.4 multiply_add_fusion.1
  53.1 1.9 collective-permute-start.3
  55.0 3.8 collective-permute-start.5
  62.4 1.2 copy.45
  65.7 2.0 copy.47
  67.7 1.9 reshape_squeeze.23
  69.6 2.0 copy.84
  78.6 101.8 %psum.21 = f32[16,8]{0,1:T(8,128)S(1)} all-reduce(f32[16,8]{0,1:T(8,128)S(1)} %fusion.2), channel_id=1, replica_groups=mesh['gx'=16,'gy'=32] {'gx','gy'}, use_global_device_ids=true, to_apply=%region_0.1 | all-reduce | flops 128 | bytes 1024 | tf_op jit(solution)/shard_map/psum | solution.py:126
  182.5 2.7 maximum_subtract_fusion
  187.6 94.6 %psum.22 = f32[16,8]{0,1:T(8,128)S(1)} all-reduce(f32[16,8]{0,1:T(8,128)S(1)} %fusion), channel_id=1, replica_groups=mesh['gx'=16,'gy'=32] {'gx','gy'}, use_global_device_ids=true, to_apply=%region_1.2 | all-reduce | flops 128 | bytes 1024 | tf_op jit(solution)/shard_map/psum | solution.py:128
  283.6 1.7 convolution_bitcast_fusion
  285.3 3.5 maximum_subtract_fusion.1
  290.8 94.3 %psum.23 = f32[8,8]{0,1:T(8,128)S(1)} all-reduce(f32[8,8]{0,1:T(8,128)S(1)} %fusion.5), channel_id=1, replica_groups=mesh['gx'=16,'gy'=32] {'gx','gy'}, use_global_device_ids=true, to_apply=%region_2.3 | all-reduce | flops 64 | bytes 512 | tf_op jit(solution)/shard_map/psum | solution.py:130
  (241 shorter events, 45.2 us)
Async XLA Ops:
  0.6 46.5 %copy-start = (f32[16,3]{0,1:T(4,128)S(1)}, f32[16,3]{0,1:T(4,128)}, u32[]{:S(2)}) copy-start(f32[16,3]{0,1:T(4,128)} %param.11) | copy-start | bytes 580
  0.6 27.3 %copy-start.1 = (f32[3,8,8,8,128]{4,3,2,1,0:T(8,128)S(1)}, f32[3,8,8,8,128]{4,3,2,1,0:T(8,128)}, u32[]{:S(2)}) copy-start(f32[3,8,8,8,128]{4,3,2,1,0:T(8,128)} %param.7) | copy-start | bytes 2359300
  2.3 47.6 %collective-permute-start.2 = (f32[3,8,1,8,128]{4,1,3,2,0:T(8,128)}, f32[3,8,1,8,128]{4,1,3,2,0:T(8,128)}, u32[]{:S(2)}, u32[]{:S(2)}) collective-permute-start(f32[3,8,1,8,128]{4,1,3,2,0:T(8,128)} %copy.105), channel_id=1, source_target_pairs={{0,32},{32,64},{64,96},{96,128},{128,160},{160,192},{192,224},{224... | collective-permute-start | bytes 294920 | tf_op jit(solution)/shard_map/ppermute | solution.py:16
  9.6 41.8 %collective-permute-start = (f32[3,8,1,8,128]{4,1,3,2,0:T(8,128)}, f32[3,8,1,8,128]{4,1,3,2,0:T(8,128)}, u32[]{:S(2)}, u32[]{:S(2)}) collective-permute-start(f32[3,8,1,8,128]{4,1,3,2,0:T(8,128)} %copy.104), channel_id=1, source_target_pairs={{32,0},{64,32},{96,64},{128,96},{160,128},{192,160},{224,192},{256... | collective-permute-start | bytes 294920 | tf_op jit(solution)/shard_map/ppermute | solution.py:17
  20.0 27.5 %collective-permute-start.4 = (s32[8,1,128]{2,0,1:T(8,128)}, s32[8,1,128]{2,0,1:T(8,128)}, u32[]{:S(2)}, u32[]{:S(2)}) collective-permute-start(s32[8,1,128]{2,0,1:T(8,128)} %bitcast.37), channel_id=1, source_target_pairs={{0,1},{1,2},{2,3},{3,4},{4,5},{5,6},{6,7},{7,8},{8,9},{9,10},{10,1... | collective-permute-start | bytes 12296 | tf_op jit(solution)/shard_map/ppermute | solution.py:25
  25.2 24.2 %collective-permute-start.1 = (s32[1,8,128]{2,1,0:T(8,128)}, s32[1,8,128]{2,1,0:T(8,128)S(1)}, u32[]{:S(2)}, u32[]{:S(2)}) collective-permute-start(s32[1,8,128]{2,1,0:T(8,128)} %slice_bitcast_fusion.72), channel_id=1, source_target_pairs={{0,32},{32,64},{64,96},{96,128},{128,160},{160,192},{192,224},{224... | collective-permute-start | bytes 12296 | tf_op jit(solution)/shard_map/ppermute | solution.py:25
  29.1 2.5 copy-start.71
  37.0 2.7 copy-start.40
  41.9 2.5 copy-start.3
  52.3 7.6 %copy-start.38 = (f32[3,8,10,8,128]{4,1,3,2,0:T(8,128)}, f32[3,8,10,8,128]{4,1,3,2,0:T(8,128)S(1)}, u32[]{:S(2)}) copy-start(f32[3,8,10,8,128]{4,1,3,2,0:T(8,128)S(1)} %get-tuple-element.112) | copy-start | bytes 2949124
  53.1 18.6 %collective-permute-start.3 = (f32[3,8,10,1,128]{4,1,3,2,0:T(8,128)}, f32[3,8,10,1,128]{4,1,3,2,0:T(8,128)}, u32[]{:S(2)}, u32[]{:S(2)}) collective-permute-start(f32[3,8,10,1,128]{4,1,3,2,0:T(8,128)} %get-tuple-element.33), channel_id=1, source_target_pairs={{1,0},{2,1},{3,2},{4,3},{5,4},{6,5},{7,6},{8,7},{9,8},{10,9},{11,1... | collective-permute-start | bytes 368648 | tf_op jit(solution)/shard_map/ppermute | solution.py:17
  55.0 16.7 %collective-permute-start.5 = (f32[3,8,10,1,128]{4,1,3,2,0:T(8,128)}, f32[3,8,10,1,128]{4,1,3,2,0:T(8,128)}, u32[]{:S(2)}, u32[]{:S(2)}) collective-permute-start(f32[3,8,10,1,128]{4,1,3,2,0:T(8,128)} %get-tuple-element.32), channel_id=1, source_target_pairs={{0,1},{1,2},{2,3},{3,4},{4,5},{5,6},{6,7},{7,8},{8,9},{9,10},{10,1... | collective-permute-start | bytes 368648 | tf_op jit(solution)/shard_map/ppermute | solution.py:16
  73.0 3.3 copy-start.28
  73.0 3.3 copy-start.29
  73.5 2.7 copy-start.30
  73.6 2.7 copy-start.31
  73.6 2.7 copy-start.32
  73.6 2.7 copy-start.33
  181.1 4.2 %copy-start.35 = (f32[1,8,8,8,128]{4,1,3,2,0:T(8,128)}, f32[1,8,8,8,128]{4,1,3,2,0:T(8,128)S(1)}, u32[]{:S(2)}) copy-start(f32[1,8,8,8,128]{4,1,3,2,0:T(8,128)S(1)} %convolution_bitcast_fusion.5) | copy-start | bytes 786436
  181.8 3.5 copy-start.36
  182.5 2.8 copy-start.37
  187.6 97.7 %copy-start.8 = (f32[1,8,8,8,128]{4,1,3,2,0:T(8,128)S(1)}, f32[1,8,8,8,128]{4,1,3,2,0:T(8,128)}, u32[]{:S(2)}) copy-start(f32[1,8,8,8,128]{4,1,3,2,0:T(8,128)} %get-tuple-element.9) | copy-start | bytes 786436
  187.6 97.7 %copy-start.11 = (f32[1,8,8,8,128]{4,1,3,2,0:T(8,128)S(1)}, f32[1,8,8,8,128]{4,1,3,2,0:T(8,128)}, u32[]{:S(2)}) copy-start(f32[1,8,8,8,128]{4,1,3,2,0:T(8,128)} %get-tuple-element.21) | copy-start | bytes 786436
  187.6 97.7 %copy-start.14 = (f32[1,8,8,8,128]{4,1,3,2,0:T(8,128)S(1)}, f32[1,8,8,8,128]{4,1,3,2,0:T(8,128)}, u32[]{:S(2)}) copy-start(f32[1,8,8,8,128]{4,1,3,2,0:T(8,128)} %get-tuple-element.22) | copy-start | bytes 786436
  (54 other events, 95.3 us)
where the time goes:
time: 393 us; the launch traced here: 392 us
  blocking collectives  291 us (74%)
  local copies, waits for them, and re-layouts  38 us (10%)
  starting transfers between devices  27.2 us (7%)
  other arithmetic  18.6 us (5%)
  matrix products  15.1 us (4%)
    psum x1, blocking collectives, per_device(): first = lax.psum(local_inner(basis, product), ('gx', 'gy')) / count  102 us
    psum x1, blocking collectives, per_device(): second = lax.psum(local_inner(basis, residual_one), ('gx', 'gy')) / count  94.6 us
    psum x1, blocking collectives, per_device(): lax.psum(local_inner(residual_two, residual_two), ('gx', 'gy')) / count  94.3 us
    unnamed x171, local copies, waits for them, and re-layouts  17.2 us
    ppermute x2, starting transfers between devices, extended(): after = lax.ppermute(leading, axis, down)  10.9 us
    ppermute x2, starting transfers between devices, extended(): before = lax.ppermute(last, axis, up)  10.5 us
  transfers between devices with their start and end apart: 6, of which 0 were waited for; matrix products, arithmetic and copies ran while one was open for 10% of the time, Pallas kernels for 0%

commit v1 on v0

--- a/solution.py
+++ b/solution.py
@@ -125,7 +125,12 @@
     width = block.shape[1]
     first = lax.psum(local_inner(basis, product), ("gx", "gy")) / count
     residual_one = product - combine(basis, first)
-    second = lax.psum(local_inner(basis, residual_one), ("gx", "gy")) / count
+
+    def process_roots(q_in):
+        block_now = jnp.sum(lax.all_gather(q_in, axis_name=("gx", "gy")), axis=0)
+        return block_now
+
+    second = process_roots(local_inner(basis, residual_one)) / count
     residual_two = residual_one - combine(basis, second)
     gram = lax.psum(local_inner(residual_two, residual_two), ("gx", "gy")) / count
     alpha = first[width:]

time: 393 us -> 984 us (2.50)
  blocking collectives: 291 us -> 880 us
    all_gather x0 -> x1, blocking collectives: none -> 684 us  [process_roots(): block_now = jnp.sum(lax.all_gather(q_in, axis_name=('gx', 'gy')), axis=0)]
    psum x1 -> x0, blocking collectives: 94.6 us -> none  [per_device(): second = lax.psum(local_inner(basis, residual_one), ('gx', 'gy')) / count]
  transfers between devices with their start and end apart: 6 -> 6, of which waited for: 0 -> 0; matrix products, arithmetic and copies ran while one was open for 10% -> 4% of each run, Pallas kernels for 0% -> 0%
where the time goes in v1:
time: 984 us; the launch traced here: 983 us
  blocking collectives  880 us (89%)
  local copies, waits for them, and re-layouts  40 us (4%)
  starting transfers between devices  27.2 us (3%)
  other arithmetic  18.9 us (2%)
  matrix products  15.1 us (2%)
    all_gather x1, blocking collectives, process_roots(): block_now = jnp.sum(lax.all_gather(q_in, axis_name=('gx', 'gy')), axis=0)  684 us
    psum x1, blocking collectives, per_device(): first = lax.psum(local_inner(basis, product), ('gx', 'gy')) / count  102 us
    psum x1, blocking collectives, per_device(): lax.psum(local_inner(residual_two, residual_two), ('gx', 'gy')) / count  93.9 us
  transfers between devices with their start and end apart: 6, of which 0 were waited for; matrix products, arithmetic and copies ran while one was open for 4% of the time, Pallas kernels for 0%

profile of v1, /device:TPU:1, one launch (start us, length us, event | category | flops | bytes accessed | tf_op | source)
XLA Modules:
  0.0 983.1 jit_solution(11507515158405790461)
XLA Ops:
  2.3 6.6 collective-permute-start.2
  9.6 9.0 collective-permute-start
  18.6 1.4 slice.453
  20.0 3.9 collective-permute-start.4
  23.9 1.3 slice_bitcast_fusion.72
  25.2 1.9 collective-permute-start.1
  32.8 1.6 copy.138
  34.4 1.3 copy.139
  37.0 1.3 copy.136
  38.3 1.3 copy.137
  42.5 1.8 multiply_add_fusion.2
  44.4 1.4 multiply_add_fusion.1
  53.0 1.9 collective-permute-start.3
  54.9 3.8 collective-permute-start.5
  67.5 2.2 copy.77
  69.7 1.9 reshape_squeeze.23
  71.6 2.0 copy.114
  73.8 1.2 multiply_add_fusion.8
  80.5 101.8 %psum.14 = f32[16,8]{0,1:T(8,128)S(1)} all-reduce(f32[16,8]{0,1:T(8,128)S(1)} %fusion.3), channel_id=1, replica_groups=mesh['gx'=16,'gy'=32] {'gx','gy'}, use_global_device_ids=true, to_apply=%region_0.1 | all-reduce | flops 128 | bytes 1024 | tf_op jit(solution)/shard_map/psum | solution.py:126
  184.5 2.9 maximum_subtract_fusion
  189.6 684.2 %all-gather.1 = f32[512,16,8]{1,2,0:T(8,128)S(1)} all-gather(f32[1,16,8]{1,2,0:T(8,128)S(1)} %fusion.1), channel_id=2, replica_groups=mesh['gx'=16,'gy'=32] {'gx','gy'}, dimensions={0}, use_global_device_ids=true | all-gather | bytes 262656 | tf_op jit(solution)/shard_map/all_gather | solution.py:130
  875.1 1.7 convolution_bitcast_fusion.1
  877.5 3.1 maximum_subtract_fusion.1
  882.7 93.9 %psum.15 = f32[8,8]{0,1:T(8,128)S(1)} all-reduce(f32[8,8]{0,1:T(8,128)S(1)} %fusion.6), channel_id=1, replica_groups=mesh['gx'=16,'gy'=32] {'gx','gy'}, use_global_device_ids=true, to_apply=%region_2.3 | all-reduce | flops 64 | bytes 512 | tf_op jit(solution)/shard_map/psum | solution.py:135
  (248 shorter events, 47.5 us)
Async XLA Ops:
  0.6 46.4 %copy-start = (f32[16,3]{0,1:T(4,128)S(1)}, f32[16,3]{0,1:T(4,128)}, u32[]{:S(2)}) copy-start(f32[16,3]{0,1:T(4,128)} %param.11) | copy-start | bytes 580
  0.6 27.3 %copy-start.1 = (f32[3,8,8,8,128]{4,3,2,1,0:T(8,128)S(1)}, f32[3,8,8,8,128]{4,3,2,1,0:T(8,128)}, u32[]{:S(2)}) copy-start(f32[3,8,8,8,128]{4,3,2,1,0:T(8,128)} %param.7) | copy-start | bytes 2359300
  2.3 47.5 %collective-permute-start.2 = (f32[3,8,1,8,128]{4,1,3,2,0:T(8,128)}, f32[3,8,1,8,128]{4,1,3,2,0:T(8,128)}, u32[]{:S(2)}, u32[]{:S(2)}) collective-permute-start(f32[3,8,1,8,128]{4,1,3,2,0:T(8,128)} %copy.135), channel_id=1, source_target_pairs={{0,32},{32,64},{64,96},{96,128},{128,160},{160,192},{192,224},{224... | collective-permute-start | bytes 294920 | tf_op jit(solution)/shard_map/ppermute | solution.py:16
  9.6 41.7 %collective-permute-start = (f32[3,8,1,8,128]{4,1,3,2,0:T(8,128)}, f32[3,8,1,8,128]{4,1,3,2,0:T(8,128)}, u32[]{:S(2)}, u32[]{:S(2)}) collective-permute-start(f32[3,8,1,8,128]{4,1,3,2,0:T(8,128)} %copy.134), channel_id=1, source_target_pairs={{32,0},{64,32},{96,64},{128,96},{160,128},{192,160},{224,192},{256... | collective-permute-start | bytes 294920 | tf_op jit(solution)/shard_map/ppermute | solution.py:17
  20.0 27.4 %collective-permute-start.4 = (s32[8,1,128]{2,0,1:T(8,128)}, s32[8,1,128]{2,0,1:T(8,128)}, u32[]{:S(2)}, u32[]{:S(2)}) collective-permute-start(s32[8,1,128]{2,0,1:T(8,128)} %bitcast.37), channel_id=1, source_target_pairs={{0,1},{1,2},{2,3},{3,4},{4,5},{5,6},{6,7},{7,8},{8,9},{9,10},{10,1... | collective-permute-start | bytes 12296 | tf_op jit(solution)/shard_map/ppermute | solution.py:25
  25.2 24.1 %collective-permute-start.1 = (s32[1,8,128]{2,1,0:T(8,128)}, s32[1,8,128]{2,1,0:T(8,128)S(1)}, u32[]{:S(2)}, u32[]{:S(2)}) collective-permute-start(s32[1,8,128]{2,1,0:T(8,128)} %slice_bitcast_fusion.72), channel_id=1, source_target_pairs={{0,32},{32,64},{64,96},{96,128},{128,160},{160,192},{192,224},{224... | collective-permute-start | bytes 12296 | tf_op jit(solution)/shard_map/ppermute | solution.py:25
  37.0 2.7 copy-start.46
  52.2 7.6 copy-start.44
  53.0 20.7 %collective-permute-start.3 = (f32[3,8,10,1,128]{4,1,3,2,0:T(8,128)}, f32[3,8,10,1,128]{4,1,3,2,0:T(8,128)}, u32[]{:S(2)}, u32[]{:S(2)}) collective-permute-start(f32[3,8,10,1,128]{4,1,3,2,0:T(8,128)} %get-tuple-element.36), channel_id=1, source_target_pairs={{1,0},{2,1},{3,2},{4,3},{5,4},{6,5},{7,6},{8,7},{9,8},{10,9},{11,1... | collective-permute-start | bytes 368648 | tf_op jit(solution)/shard_map/ppermute | solution.py:17
  54.9 18.8 %collective-permute-start.5 = (f32[3,8,10,1,128]{4,1,3,2,0:T(8,128)}, f32[3,8,10,1,128]{4,1,3,2,0:T(8,128)}, u32[]{:S(2)}, u32[]{:S(2)}) collective-permute-start(f32[3,8,10,1,128]{4,1,3,2,0:T(8,128)} %get-tuple-element.35), channel_id=1, source_target_pairs={{0,1},{1,2},{2,3},{3,4},{4,5},{5,6},{6,7},{7,8},{8,9},{9,10},{10,1... | collective-permute-start | bytes 368648 | tf_op jit(solution)/shard_map/ppermute | solution.py:16
  67.5 115.6 %copy-start.5 = (f32[2,8,64,128]{3,2,1,0:T(8,128)}, f32[2,8,64,128]{3,2,1,0:T(8,128)S(1)}, u32[]{:S(2)}) copy-start(f32[2,8,64,128]{3,2,1,0:T(8,128)S(1)} %copy.113) | copy-start | bytes 1572868
  75.0 3.1 copy-start.34
  75.1 3.1 copy-start.35
  75.6 2.6 copy-start.36
  183.0 4.3 copy-start.41
  183.7 3.6 copy-start.42
  184.4 2.9 copy-start.43
  874.3 3.1 copy-start.10
  874.3 3.1 copy-start.13
  874.3 3.1 copy-start.16
  874.4 3.1 copy-start.19
  874.4 3.1 copy-start.22
  874.4 3.1 copy-start.25
  874.4 3.1 copy-start.28
  (57 other events, 103.5 us)
